TPU v7x, 32 devices: a whole 2x2x4 slice. The times are simulated.
32 devices in a mesh: node: 4 (over y, core), cores: 8 (over z, x).
Axes of the slice: x: 2, y: 2, z: 4, core: 2. Of those that a mesh axis runs over, the one named last changes fastest.
Arguments:
- adjoint: bfloat16 [256, 2, 128, 128], P(('node', 'cores')), may hold values from -6 to 6
- saved: bfloat16 [2, 4, 256, 2, 128, 128], P(None, None, ('node', 'cores')), may hold values from -0.046875 to 0.046875
- propagators: bfloat16 [2, 4, 2, 128, 128], replicated, may hold values from -3 to 3, as said below
- coupling: bfloat16 [128, 128], replicated, may hold values from -0.5 to 0.5
- higher: int32 [256, 4], replicated, may hold values from 0 to 255, as said below
- lower: int32 [256, 4], replicated, may hold values from 0 to 255, as said below
- ladder: int32 [2, 256, 4], P(None, ('node', 'cores')), may hold values from 0 to 3
- rates: float32 [2, 4], replicated, may hold values from 0.1 to 0.4
- decay: float32 [256], P(('node', 'cores')), may hold values from 0.4 to 1
Outputs:
- adjoint_out: bfloat16 [256, 2, 128, 128], P(('node', 'cores'))
- gradient: float32 [128, 8, 2, 128], P(('node', 'cores'))
Inputs may be any that keep to these rules, and one draw needn't show every extreme that they name: Density j lives on owner j // 8. Taken in the order of density then mode, the 32 higher-tier partners of one owner's densities lie on distinct owners when 8 * 4 <= 32, and else exactly 1 of them lie on each owner. The same holds for the lower-tier partners. `propagators`: A propagator substep is close to unitary.
All inputs are finite; a program needn't handle non-finite values.
Results may differ from a plain program's by a relative error of at most 0.024.
Values may be sent and summed in bfloat16 or wider, within the bound.
A program may use at most 128 MiB of HBM per device.

v0:
```python
import jax
import jax.numpy as jnp
from jax import lax
from jax.sharding import PartitionSpec as P


def send_slots(link_table, owners, own_index, own_count, links, capacity):
    flattened = link_table.reshape(owners, links)
    source = flattened // own_count
    local = flattened % own_count
    mine = (source == own_index).astype(jnp.int32)
    before = jnp.cumsum(mine, axis=1) - mine
    picked = [jnp.sum(jnp.where((mine == 1) & (before == 0), local, 0), axis=1)]
    return jnp.stack(picked, axis=1).reshape(owners * capacity)


def receive_slots(link_table, own_index, own_count, links, capacity):
    own_rows = lax.dynamic_slice_in_dim(link_table, own_index * own_count, own_count, 0).reshape(
        links
    )
    source = own_rows // own_count
    positions = jnp.arange(links)
    earlier = (source[:, None] == source[None, :]) & (positions[None, :] < positions[:, None])
    before = jnp.sum(earlier.astype(jnp.int32), axis=1)
    return source * capacity + before


def linked_sum(received, picks, weights, strengths, own_count, modes):
    chosen = received[picks].reshape((own_count, modes) + received.shape[1:])
    factors = weights.astype(jnp.float32) * strengths[None, :]
    total = factors[:, 0, None, None, None] * chosen[:, 0].astype(jnp.float32)
    for mode_index in range(1, modes):
        total = total + factors[:, mode_index, None, None, None] * chosen[:, mode_index].astype(
            jnp.float32
        )
    return total


def couple_step(state, up_sum, down_sum, coupling, decay):
    plus = (up_sum + down_sum).astype(jnp.bfloat16)
    minus = (up_sum - down_sum).astype(jnp.bfloat16)
    left = jnp.einsum("ab,jxbc->jxac", coupling, plus, preferred_element_type=jnp.float32)
    right = jnp.einsum("jxab,bc->jxac", minus, coupling, preferred_element_type=jnp.float32)
    kept = decay[:, None, None, None] * state.astype(jnp.float32)
    real_part = kept[:, 0] + left[:, 1] - right[:, 1]
    imag_part = kept[:, 1] - left[:, 0] + right[:, 0]
    return jnp.stack([real_part, imag_part], axis=1).astype(jnp.bfloat16)


def rotate_step(state, prop_re, prop_im):
    times_re = jnp.einsum("jxab,bc->jxac", state, prop_re, preferred_element_type=jnp.float32)
    times_im = jnp.einsum("jxab,bc->jxac", state, prop_im, preferred_element_type=jnp.float32)
    middle = jnp.stack(
        [times_re[:, 0] - times_im[:, 1], times_im[:, 0] + times_re[:, 1]], axis=1
    ).astype(jnp.bfloat16)
    left_re = jnp.einsum("ba,jxbc->jxac", prop_re, middle, preferred_element_type=jnp.float32)
    left_im = jnp.einsum("ba,jxbc->jxac", prop_im, middle, preferred_element_type=jnp.float32)
    result = jnp.stack([left_re[:, 0] + left_im[:, 1], left_re[:, 1] - left_im[:, 0]], axis=1)
    return result.astype(jnp.bfloat16)


def projection(saved_block, state):
    swapped = jnp.stack([state[:, 1], -state[:, 0]], axis=1)
    real_part = jnp.einsum("jxba,jxbc->ac", saved_block, state, preferred_element_type=jnp.float32)
    imag_part = jnp.einsum(
        "jxba,jxbc->ac", saved_block, swapped, preferred_element_type=jnp.float32
    )
    return jnp.stack([real_part, imag_part], axis=1)


def body(adjoint, saved, propagators, coupling, higher, lower, ladder, rates, decay):
    owners = lax.axis_size(("node", "cores"))
    own_index = lax.axis_index(("node", "cores"))
    own_count = adjoint.shape[0]
    modes = higher.shape[1]
    links = own_count * modes
    capacity = max(1, links // owners)
    step_count = propagators.shape[0]
    sub_count = propagators.shape[1]
    grad_rows = coupling.shape[0] // owners
    up_send = send_slots(higher, owners, own_index, own_count, links, capacity)
    down_send = send_slots(lower, owners, own_index, own_count, links, capacity)
    up_take = receive_slots(higher, own_index, own_count, links, capacity)
    down_take = receive_slots(lower, own_index, own_count, links, capacity)
    state = adjoint
    pieces = []
    for step_index in range(step_count):
        up_out = state[up_send]
        down_out = state[down_send]
        up_in, down_in = (
            lax.all_to_all(up_out, ("node", "cores"), split_axis=0, concat_axis=0, tiled=True),
            lax.all_to_all(down_out, ("node", "cores"), split_axis=0, concat_axis=0, tiled=True),
        )
        up_sum = linked_sum(up_in, up_take, ladder[0], rates[0], own_count, modes)
        down_sum = linked_sum(down_in, down_take, ladder[1], rates[1], own_count, modes)
        state = couple_step(state, up_sum, down_sum, coupling, decay)
        step_terms = []
        for substep in range(sub_count):
            state = rotate_step(
                state, propagators[step_index, substep, 0], propagators[step_index, substep, 1]
            )
            step_terms.append(projection(saved[step_index, substep], state))
        terms = jnp.stack(step_terms, axis=1)

        def step_rows(first_row, row_count, terms=terms):
            return terms

        pieces.append(
            lax.psum_scatter(
                step_rows(jnp.int32(0), grad_rows * lax.axis_size(("node", "cores"))),
                ("node", "cores"),
                scatter_dimension=0,
                tiled=True,
            )
        )
    gradient = jnp.concatenate(pieces, axis=1)
    return (state, gradient)


def solution(mesh):
    return jax.shard_map(
        body,
        mesh=mesh,
        in_specs=(
            P(("node", "cores"), None, None, None),
            P(None, None, ("node", "cores"), None, None, None),
            P(),
            P(),
            P(),
            P(),
            P(None, ("node", "cores"), None),
            P(),
            P(("node", "cores")),
        ),
        out_specs=(P(("node", "cores"), None, None, None), P(("node", "cores"), None, None, None)),
        check_vma=False,
    )
```

profile of v0, /device:TPU:0, one launch (start us, length us, event | category | flops | bytes accessed | tf_op | source)
XLA Modules:
  0.0 418.2 jit_solution(13472476273599441604)
XLA Ops:
  7.2 0.9 copy.231
  8.1 0.7 broadcast_compare_fusion.1
  8.8 0.8 copy.245
  9.6 0.7 broadcast_compare_fusion
  11.5 0.4 fusion.126
  12.1 2.2 gather_fusion.2
  14.3 7.3 %all-to-all-start.1 = ((bf16[32,2,128,128]{3,2,1,0:T(8,128)(2,1)}), bf16[32,2,128,128]{3,2,1,0:T(8,128)(2,1)S(1)}, u32[]{:S(2)}, u32[]{:S(2)}) async-start(bf16[32,2,128,128]{3,2,1,0:T(8,128)(2,1)} %gather_fusion.2), calls=%async_computation.1 | async-start | bytes 4194304 | tf_op jit(solution)/shard_map/all_to_all | solution.py:92
  21.9 2.1 gather_fusion
  24.0 47.5 %all-to-all-done.1 = bf16[32,2,128,128]{3,2,1,0:T(8,128)(2,1)S(1)} async-done(((bf16[32,2,128,128]{3,2,1,0:T(8,128)(2,1)}), bf16[32,2,128,128]{3,2,1,0:T(8,128)(2,1)S(1)}, u32[]{:S(2)}, u32[]{:S(2)}) %all-to-all-start.1) | async-done | bytes 2097184 | tf_op jit(solution)/shard_map/all_to_all | solution.py:92
  71.6 3.5 all-to-all-start
  76.6 1.1 convert_multiply_fusion.17
  77.7 2.2 gather_fusion.3
  79.9 45.1 %all-to-all-done = bf16[32,2,128,128]{3,2,1,0:T(8,128)(2,1)} async-done(((bf16[32,2,128,128]{3,2,1,0:T(8,128)(2,1)}), bf16[32,2,128,128]{3,2,1,0:T(8,128)(2,1)}, u32[]{:S(2)}, u32[]{:S(2)}) %all-to-all-start) | async-done | bytes 2097184 | tf_op jit(solution)/shard_map/all_to_all | solution.py:91
  125.0 3.7 gather_fusion.1
  128.7 2.6 convolution_bitcast_fusion.17
  131.3 2.7 fusion.12
  134.2 0.8 copy-done.14
  135.4 0.3 fusion.108
  135.8 0.3 convolution_bitcast_fusion.16
  136.2 0.3 convolution_bitcast_fusion.15
  136.5 0.8 fusion.272
  137.4 0.3 fusion.121
  138.8 0.3 convolution_bitcast_fusion.13
  139.2 0.8 fusion.274
  141.9 0.8 fusion.276
  144.5 0.8 fusion.278
  145.4 0.7 copy-done.9
  146.2 2.1 gather_fusion.6
  148.3 2.9 all-to-all-start.3
  151.3 2.2 gather_fusion.4
  153.4 47.8 %all-to-all-done.3 = bf16[32,2,128,128]{2,3,1,0:T(8,128)(2,1)S(1)} async-done(((bf16[32,2,128,128]{2,3,1,0:T(8,128)(2,1)}), bf16[32,2,128,128]{2,3,1,0:T(8,128)(2,1)S(1)}, u32[]{:S(2)}, u32[]{:S(2)}) %all-to-all-start.3) | async-done | bytes 2097184 | tf_op jit(solution)/shard_map/all_to_all | solution.py:92
  201.2 1.3 copy-done.2
  202.5 3.0 all-to-all-start.2
  205.8 1.6 convolution_bitcast_fusion.31
  207.3 1.5 convolution_bitcast_fusion.30
  208.8 1.4 convolution_bitcast_fusion.29
  212.3 1.0 copy.305
  213.3 1.1 convert_multiply_fusion.16
  214.4 3.8 gather_fusion.7
  218.2 2.9 fusion.288
  221.0 2.1 copy.390
  223.1 2.1 copy.391
  225.2 2.0 copy.392
  227.2 2.0 copy.393
  229.2 26.2 %all-to-all-done.2 = bf16[32,2,128,128]{2,3,1,0:T(8,128)(2,1)S(1)} async-done(((bf16[32,2,128,128]{2,3,1,0:T(8,128)(2,1)}), bf16[32,2,128,128]{2,3,1,0:T(8,128)(2,1)S(1)}, u32[]{:S(2)}, u32[]{:S(2)}) %all-to-all-start.2) | async-done | bytes 2097184 | tf_op jit(solution)/shard_map/all_to_all | solution.py:91
  255.4 2.2 gather_fusion.5
  257.6 1.7 fusion.289
  259.3 1.0 copy.386
  260.3 1.0 copy.387
  261.3 1.0 copy.388
  262.7 2.9 convolution_bitcast_fusion.8
  265.7 1.1 fusion.13
  266.9 0.8 copy-done.15
  268.9 0.3 convolution_bitcast_fusion.6
  269.4 1.7 copy-done.33
  274.1 0.3 convolution_bitcast_fusion.3
  274.5 0.3 convolution_bitcast_fusion.2
  275.0 0.5 convolution_bitcast_fusion.21
  278.7 1.0 copy.306
  279.8 1.0 copy.307
  280.8 128.5 %all-reduce.5.cloned.1.call-done = (f32[128,4,2,128]{3,1,2,0:T(4,128)}, f32[128,4,2,128]{3,1,2,0:T(4,128)}) async-done(((f32[128,4,2,128]{3,1,2,0:T(4,128)}, f32[128,4,2,128]{3,1,2,0:T(4,128)}), (f32[128,4,2,128]{3,1,2,0:T(4,128)}, f32[128,4,2,128]{3,1,2,0:T(4,128)})) %all-reduce.5.cloned.1.call-update) | async-done | bytes 1048592
  409.3 0.7 constant_dynamic-slice_fusion
  410.0 0.7 constant_dynamic-slice_fusion.1
  410.8 0.6 copy.308
  (174 shorter events, 18.9 us)
Async XLA Ops:
  7.2 121.5 %copy-start = (bf16[128,128]{1,0:T(8,128)(2,1)S(1)}, bf16[128,128]{1,0:T(8,128)(2,1)}, u32[]{:S(2)}) copy-start(bf16[128,128]{1,0:T(8,128)(2,1)} %param.12) | copy-start | bytes 98308
  7.2 4.9 %copy-start.1 = (bf16[8,2,128,128]{3,2,1,0:T(8,128)(2,1)S(1)}, bf16[8,2,128,128]{3,2,1,0:T(8,128)(2,1)}, u32[]{:S(2)}) copy-start(bf16[8,2,128,128]{3,2,1,0:T(8,128)(2,1)} %param.9) | copy-start | bytes 1572868
  14.3 57.3 %all-to-all-start.1 = ((bf16[32,2,128,128]{3,2,1,0:T(8,128)(2,1)}), bf16[32,2,128,128]{3,2,1,0:T(8,128)(2,1)S(1)}, u32[]{:S(2)}, u32[]{:S(2)}) async-start(bf16[32,2,128,128]{3,2,1,0:T(8,128)(2,1)} %gather_fusion.2), calls=%async_computation.1 | async-start | bytes 4194304 | tf_op jit(solution)/shard_map/all_to_all | solution.py:92
  24.0 51.0 %copy-start.27 = (s32[256,4]{0,1:T(4,128)S(1)}, s32[256,4]{0,1:T(4,128)}, u32[]{:S(2)}) copy-start(s32[256,4]{0,1:T(4,128)} %param.14) | copy-start | bytes 12292
  24.0 51.4 %copy-start.28 = (s32[256,4]{0,1:T(4,128)S(1)}, s32[256,4]{0,1:T(4,128)}, u32[]{:S(2)}) copy-start(s32[256,4]{0,1:T(4,128)} %param.13) | copy-start | bytes 12292
  24.0 52.4 %copy-start.31 = (f32[2,4]{1,0:T(2,128)S(1)}, f32[2,4]{1,0:T(2,128)}, u32[]{:S(2)}) copy-start(f32[2,4]{1,0:T(2,128)} %param.16) | copy-start | bytes 100
  24.0 52.5 %copy-start.29 = (s32[2,8,4]{1,2,0:T(4,128)S(1)}, s32[2,8,4]{1,2,0:T(4,128)}, u32[]{:S(2)}) copy-start(s32[2,8,4]{1,2,0:T(4,128)} %param.15) | copy-start | bytes 772
  24.0 52.5 %copy-start.30 = (f32[8]{0:T(128)S(1)}, f32[8]{0:T(128)}, u32[]{:S(2)}) copy-start(f32[8]{0:T(128)} %param.17) | copy-start | bytes 100
  71.6 53.4 %all-to-all-start = ((bf16[32,2,128,128]{3,2,1,0:T(8,128)(2,1)}), bf16[32,2,128,128]{3,2,1,0:T(8,128)(2,1)}, u32[]{:S(2)}, u32[]{:S(2)}) async-start(bf16[32,2,128,128]{3,2,1,0:T(8,128)(2,1)} %gather_fusion), calls=%async_computation | async-start | bytes 4194304 | tf_op jit(solution)/shard_map/all_to_all | solution.py:91
  79.9 48.8 %copy-start.16 = (bf16[32,2,128,128]{3,2,1,0:T(8,128)(2,1)S(1)}, bf16[32,2,128,128]{3,2,1,0:T(8,128)(2,1)}, u32[]{:S(2)}) copy-start(bf16[32,2,128,128]{3,2,1,0:T(8,128)(2,1)} %gather_fusion.3) | copy-start | bytes 6291460
  131.3 2.7 copy-start.3
  134.0 1.0 copy-start.14
  137.3 0.7 copy-start.4
  140.0 0.7 copy-start.6
  142.7 0.7 copy-start.7
  145.3 3.0 copy-start.12
  145.4 0.7 copy-start.9
  148.3 52.9 %all-to-all-start.3 = ((bf16[32,2,128,128]{2,3,1,0:T(8,128)(2,1)}), bf16[32,2,128,128]{2,3,1,0:T(8,128)(2,1)S(1)}, u32[]{:S(2)}, u32[]{:S(2)}) async-start(bf16[32,2,128,128]{2,3,1,0:T(8,128)(2,1)} %gather_fusion.6), calls=%async_computation.3 | async-start | bytes 4194304 | tf_op jit(solution)/shard_map/all_to_all | solution.py:92
  201.2 1.3 copy-start.2
  202.5 52.9 %all-to-all-start.2 = ((bf16[32,2,128,128]{2,3,1,0:T(8,128)(2,1)}), bf16[32,2,128,128]{2,3,1,0:T(8,128)(2,1)S(1)}, u32[]{:S(2)}, u32[]{:S(2)}) async-start(bf16[32,2,128,128]{2,3,1,0:T(8,128)(2,1)} %gather_fusion.4), calls=%async_computation.2 | async-start | bytes 4194304 | tf_op jit(solution)/shard_map/all_to_all | solution.py:91
  205.5 3.3 copy-start.8
  205.5 203.8 %all-reduce.5.cloned.1.call-start = ((), (), s32[]{:S(2)}) async-start(), calls=%async_computation.4 | async-start | bytes 2097152
  205.7 4.5 %copy-start.32 = (bf16[2,4,8,2,128,128]{5,4,3,2,1,0:T(8,128)(2,1)S(1)}, bf16[2,4,8,2,128,128]{5,4,3,2,1,0:T(8,128)(2,1)}, u32[]{:S(2)}) copy-start(bf16[2,4,8,2,128,128]{5,4,3,2,1,0:T(8,128)(2,1)} %param.10) | copy-start | bytes 12582916
  207.3 2.9 copy-start.25
  208.8 1.8 copy-start.10
  208.8 1.8 copy-start.13
  210.2 1.0 copy-start.26
  210.6 1.0 copy-start.5
  210.9 1.0 copy-start.24
  211.8 1.4 copy-start.11
  260.3 2.3 copy-start.17
  261.3 1.3 copy-start.18
  262.6 3.0 copy-start.19
  262.6 3.0 copy-start.20
  262.7 3.0 copy-start.21
  262.7 3.0 copy-start.22
  262.7 3.0 copy-start.23
  266.7 1.0 copy-start.15
  268.9 2.2 copy-start.33
Sparse Core Ops, SparseCore 0:
  279.9 129.3 all-reduce.4
where the time goes:
time: 419 us; the launch traced here: 418 us
  waiting for transfers between devices  295 us (70%)
  local copies, waits for them, and re-layouts  52 us (12%)
  matrix products  28.2 us (7%)
  starting transfers between devices  16.9 us (4%)
  between operations  15.1 us (4%)
  other arithmetic  11 us (3%)
    unnamed x2, waiting for transfers between devices  128 us
    all_to_all x2, waiting for transfers between devices, body(): lax.all_to_all(down_out, ('node', 'cores'), split_axis=0, concat_axis=0,...  95.3 us
    all_to_all x2, waiting for transfers between devices, body(): lax.all_to_all(up_out, ('node', 'cores'), split_axis=0, concat_axis=0, ti...  71.3 us
    unnamed x83, local copies, waits for them, and re-layouts  23.4 us
    gather x4, local copies, waits for them, and re-layouts, linked_sum(): chosen = received[picks].reshape((own_count, modes) + received.shape[1:])  11.9 us
    all_to_all x2, starting transfers between devices, body(): lax.all_to_all(down_out, ('node', 'cores'), split_axis=0, concat_axis=0,...  10.2 us
  transfers between devices with their start and end apart: 5, of which 5 were waited for; matrix products, arithmetic and copies ran while one was open for 8% of the time, Pallas kernels for 0%

commit v1 on v0

--- a/solution.py
+++ b/solution.py
@@ -100,19 +100,12 @@
                 state, propagators[step_index, substep, 0], propagators[step_index, substep, 1]
             )
             step_terms.append(projection(saved[step_index, substep], state))
-        terms = jnp.stack(step_terms, axis=1)
-
-        def step_rows(first_row, row_count, terms=terms):
-            return terms
-
-        pieces.append(
-            lax.psum_scatter(
-                step_rows(jnp.int32(0), grad_rows * lax.axis_size(("node", "cores"))),
-                ("node", "cores"),
-                scatter_dimension=0,
-                tiled=True,
-            )
+        terms = jnp.stack(step_terms, axis=1).astype(jnp.bfloat16)
+        swapped = lax.all_to_all(
+            terms, ("node", "cores"), split_axis=0, concat_axis=0, tiled=True
         )
+        by_owner = swapped.reshape((owners, grad_rows) + swapped.shape[1:])
+        pieces.append(jnp.sum(by_owner.astype(jnp.float32), axis=0))
     gradient = jnp.concatenate(pieces, axis=1)
     return (state, gradient)
 

time: 419 us -> 294 us (0.70)
  waiting for transfers between devices: 295 us -> 176 us
  between operations: 15.1 us -> 1.74 us
  starting transfers between devices: 16.9 us -> 25.7 us
    unnamed x2 -> x0, waiting for transfers between devices: 128 us -> none
    all_to_all x2, waiting for transfers between devices: 71.3 us -> 92.7 us  [body(): lax.all_to_all(up_out, ('node', 'cores'), split_axis=0, concat_axis=0, ti...]
    all_to_all x2, waiting for transfers between devices: 95.3 us -> 74.1 us  [body(): lax.all_to_all(down_out, ('node', 'cores'), split_axis=0, concat_axis=0,...]
    all_to_all x0 -> x2, waiting for transfers between devices: none -> 9.21 us  [body(): lax.all_to_all(terms, ('node', 'cores'), split_axis=0, concat_axis=0, til...]
    all_to_all x0 -> x2, starting transfers between devices: none -> 8.79 us  [body(): lax.all_to_all(terms, ('node', 'cores'), split_axis=0, concat_axis=0, til...]
    unnamed x83 -> x81, local copies, waits for them, and re-layouts: 23.4 us -> 21.3 us
  transfers between devices with their start and end apart: 5 -> 6, of which waited for: 5 -> 5; matrix products, arithmetic and copies ran while one was open for 8% -> 19% of each run, Pallas kernels for 0% -> 0%
where the time goes in v1:
time: 294 us; the launch traced here: 292 us
  waiting for transfers between devices  176 us (60%)
  local copies, waits for them, and re-layouts  49.7 us (17%)
  matrix products  28 us (10%)
  starting transfers between devices  25.7 us (9%)
  other arithmetic  11.2 us (4%)
    all_to_all x2, waiting for transfers between devices, body(): lax.all_to_all(up_out, ('node', 'cores'), split_axis=0, concat_axis=0, ti...  92.7 us
    all_to_all x2, waiting for transfers between devices, body(): lax.all_to_all(down_out, ('node', 'cores'), split_axis=0, concat_axis=0,...  74.1 us
    unnamed x81, local copies, waits for them, and re-layouts  21.3 us
    gather x4, local copies, waits for them, and re-layouts, linked_sum(): chosen = received[picks].reshape((own_count, modes) + received.shape[1:])  11.9 us
    all_to_all x2, starting transfers between devices, body(): lax.all_to_all(down_out, ('node', 'cores'), split_axis=0, concat_axis=0,...  10.3 us
    all_to_all x2, waiting for transfers between devices, body(): lax.all_to_all(terms, ('node', 'cores'), split_axis=0, concat_axis=0, til...  9.21 us
    all_to_all x2, starting transfers between devices, body(): lax.all_to_all(terms, ('node', 'cores'), split_axis=0, concat_axis=0, til...  8.79 us
    all_to_all x2, starting transfers between devices, body(): lax.all_to_all(up_out, ('node', 'cores'), split_axis=0, concat_axis=0, ti...  6.59 us
  transfers between devices with their start and end apart: 6, of which 5 were waited for; matrix products, arithmetic and copies ran while one was open for 19% of the time, Pallas kernels for 0%

profile of v1, /device:TPU:0, one launch (start us, length us, event | category | flops | bytes accessed | tf_op | source)
XLA Modules:
  0.0 292.4 jit_solution(10761097293361201043)
XLA Ops:
  0.7 0.8 broadcast_compare_fusion.1
  1.4 0.8 copy.233
  2.2 0.7 broadcast_compare_fusion
  2.9 0.8 copy.247
  5.0 0.4 fusion.158
  5.6 2.2 gather_fusion.2
  7.8 7.3 %all-to-all-start.1 = ((bf16[32,2,128,128]{3,2,1,0:T(8,128)(2,1)}), bf16[32,2,128,128]{3,2,1,0:T(8,128)(2,1)S(1)}, u32[]{:S(2)}, u32[]{:S(2)}) async-start(bf16[32,2,128,128]{3,2,1,0:T(8,128)(2,1)} %gather_fusion.2), calls=%async_computation.1 | async-start | bytes 4194304 | tf_op jit(solution)/shard_map/all_to_all | solution.py:92
  15.3 2.2 gather_fusion
  17.5 47.5 %all-to-all-done.1 = bf16[32,2,128,128]{3,2,1,0:T(8,128)(2,1)S(1)} async-done(((bf16[32,2,128,128]{3,2,1,0:T(8,128)(2,1)}), bf16[32,2,128,128]{3,2,1,0:T(8,128)(2,1)S(1)}, u32[]{:S(2)}, u32[]{:S(2)}) %all-to-all-start.1) | async-done | bytes 2097184 | tf_op jit(solution)/shard_map/all_to_all | solution.py:92
  65.0 3.5 %all-to-all-start = ((bf16[32,2,128,128]{3,2,1,0:T(8,128)(2,1)}), bf16[32,2,128,128]{3,2,1,0:T(8,128)(2,1)}, u32[]{:S(2)}, u32[]{:S(2)}) async-start(bf16[32,2,128,128]{3,2,1,0:T(8,128)(2,1)} %gather_fusion), calls=%async_computation | async-start | bytes 4194304 | tf_op jit(solution)/shard_map/all_to_all | solution.py:91
  70.0 1.1 convert_multiply_fusion.17
  71.2 2.2 gather_fusion.3
  73.4 45.1 %all-to-all-done = bf16[32,2,128,128]{3,2,1,0:T(8,128)(2,1)} async-done(((bf16[32,2,128,128]{3,2,1,0:T(8,128)(2,1)}), bf16[32,2,128,128]{3,2,1,0:T(8,128)(2,1)}, u32[]{:S(2)}, u32[]{:S(2)}) %all-to-all-start) | async-done | bytes 2097184 | tf_op jit(solution)/shard_map/all_to_all | solution.py:91
  118.4 3.7 %gather_fusion.1 = bf16[32,2,128,128]{3,2,1,0:T(8,128)(2,1)} fusion(bf16[32,2,128,128]{3,2,1,0:T(8,128)(2,1)} %all-to-all-done, s32[1024]{0:T(1024)S(1)} %pad_clamp_fusion.2), kind=kCustom, calls=%fused_computation.1 | custom fusion | bytes 4194432 | tf_op jit(solution)/shard_map/gather | solution.py:29
  122.2 2.6 fusion.44
  124.8 2.7 convolution_bitcast_fusion.17
  127.7 0.8 copy-done.14
  128.9 0.3 fusion.141
  129.3 0.3 convolution_bitcast_fusion.15
  129.7 0.3 convolution_bitcast_fusion.16
  130.1 0.8 fusion.304
  131.2 0.4 copy-done.4
  132.4 0.3 convolution_bitcast_fusion.14
  132.8 0.8 fusion.306
  133.9 0.4 copy-done.5
  135.5 0.8 fusion.308
  136.7 0.4 copy-done.7
  138.2 0.8 fusion.310
  139.1 2.2 gather_fusion.4
  141.3 3.1 %all-to-all-start.2 = ((bf16[32,2,128,128]{2,3,1,0:T(8,128)(2,1)}), bf16[32,2,128,128]{2,3,1,0:T(8,128)(2,1)S(1)}, u32[]{:S(2)}, u32[]{:S(2)}) async-start(bf16[32,2,128,128]{2,3,1,0:T(8,128)(2,1)} %gather_fusion.4), calls=%async_computation.2 | async-start | bytes 4194304 | tf_op jit(solution)/shard_map/all_to_all | solution.py:91
  144.4 2.2 gather_fusion.6
  146.6 47.6 %all-to-all-done.2 = bf16[32,2,128,128]{2,3,1,0:T(8,128)(2,1)S(1)} async-done(((bf16[32,2,128,128]{2,3,1,0:T(8,128)(2,1)}), bf16[32,2,128,128]{2,3,1,0:T(8,128)(2,1)S(1)}, u32[]{:S(2)}, u32[]{:S(2)}) %all-to-all-start.2) | async-done | bytes 2097184 | tf_op jit(solution)/shard_map/all_to_all | solution.py:91
  194.1 1.3 copy-done.2
  195.5 3.0 %all-to-all-start.3 = ((bf16[32,2,128,128]{2,3,1,0:T(8,128)(2,1)}), bf16[32,2,128,128]{2,3,1,0:T(8,128)(2,1)S(1)}, u32[]{:S(2)}, u32[]{:S(2)}) async-start(bf16[32,2,128,128]{2,3,1,0:T(8,128)(2,1)} %gather_fusion.6), calls=%async_computation.3 | async-start | bytes 4194304 | tf_op jit(solution)/shard_map/all_to_all | solution.py:92
  198.5 1.6 fusion.31
  200.0 1.5 fusion.30
  201.6 1.4 fusion.29
  205.0 0.9 copy.307
  205.9 1.1 convert_multiply_fusion.16
  207.0 3.8 %gather_fusion.5 = bf16[32,2,128,128]{2,3,1,0:T(8,128)(2,1)} fusion(bf16[32,2,128,128]{2,3,1,0:T(8,128)(2,1)} %copy-done.2, s32[1024]{0:T(1024)S(1)} %pad_clamp_fusion.2), kind=kCustom, calls=%fused_computation.5 | custom fusion | bytes 4194432 | tf_op jit(solution)/shard_map/gather | solution.py:29
  210.8 2.9 fusion.321
  213.7 2.0 copy.390
  215.7 2.0 copy.392
  217.7 2.0 copy.391
  219.8 2.0 copy.393
  221.8 26.6 %all-to-all-done.3 = bf16[32,2,128,128]{2,3,1,0:T(8,128)(2,1)S(1)} async-done(((bf16[32,2,128,128]{2,3,1,0:T(8,128)(2,1)}), bf16[32,2,128,128]{2,3,1,0:T(8,128)(2,1)S(1)}, u32[]{:S(2)}, u32[]{:S(2)}) %all-to-all-start.3) | async-done | bytes 2097184 | tf_op jit(solution)/shard_map/all_to_all | solution.py:92
  248.4 3.0 %all-to-all-start.4 = ((bf16[128,4,2,128]{3,2,1,0:T(2,128)(2,1)}), bf16[128,4,2,128]{3,2,1,0:T(2,128)(2,1)S(1)}, u32[]{:S(2)}, u32[]{:S(2)}) async-start(bf16[128,4,2,128]{3,2,1,0:T(2,128)(2,1)} %copy.307), calls=%async_computation.4 | async-start | bytes 524288 | tf_op jit(solution)/shard_map/all_to_all | solution.py:104
  251.4 2.2 gather_fusion.7
  253.5 1.7 fusion.320
  255.2 1.0 copy.394
  256.2 1.0 copy.396
  257.2 1.0 copy.395
  258.6 2.9 fusion.45
  261.5 1.1 convolution_bitcast_fusion.8
  262.8 0.8 copy-done.15
  264.5 0.3 convolution_bitcast_fusion.6
  265.3 1.7 copy-done.33
  269.2 0.3 fusion.144
  269.6 0.3 fusion.145
  274.4 0.9 copy.309
  275.3 5.8 %all-to-all-start.5 = ((bf16[128,4,2,128]{3,2,1,0:T(2,128)(2,1)}), bf16[128,4,2,128]{3,2,1,0:T(2,128)(2,1)S(1)}, u32[]{:S(2)}, u32[]{:S(2)}) async-start(bf16[128,4,2,128]{3,2,1,0:T(2,128)(2,1)} %copy.309), calls=%async_computation.5 | async-start | bytes 524288 | tf_op jit(solution)/shard_map/all_to_all | solution.py:104
  281.3 1.0 copy.311
  282.3 9.2 %all-to-all-done.5 = bf16[128,4,2,128]{3,2,1,0:T(2,128)(2,1)S(1)} async-done(((bf16[128,4,2,128]{3,2,1,0:T(2,128)(2,1)}), bf16[128,4,2,128]{3,2,1,0:T(2,128)(2,1)S(1)}, u32[]{:S(2)}, u32[]{:S(2)}) %all-to-all-start.5) | async-done | bytes 262176 | tf_op jit(solution)/shard_map/all_to_all | solution.py:104
  291.7 0.6 copy.312
  (177 shorter events, 18.6 us)
Async XLA Ops:
  0.6 121.6 %copy-start = (bf16[128,128]{1,0:T(8,128)(2,1)S(1)}, bf16[128,128]{1,0:T(8,128)(2,1)}, u32[]{:S(2)}) copy-start(bf16[128,128]{1,0:T(8,128)(2,1)} %param.12) | copy-start | bytes 98308
  0.6 4.9 %copy-start.1 = (bf16[8,2,128,128]{3,2,1,0:T(8,128)(2,1)S(1)}, bf16[8,2,128,128]{3,2,1,0:T(8,128)(2,1)}, u32[]{:S(2)}) copy-start(bf16[8,2,128,128]{3,2,1,0:T(8,128)(2,1)} %param.9) | copy-start | bytes 1572868
  7.8 57.3 %all-to-all-start.1 = ((bf16[32,2,128,128]{3,2,1,0:T(8,128)(2,1)}), bf16[32,2,128,128]{3,2,1,0:T(8,128)(2,1)S(1)}, u32[]{:S(2)}, u32[]{:S(2)}) async-start(bf16[32,2,128,128]{3,2,1,0:T(8,128)(2,1)} %gather_fusion.2), calls=%async_computation.1 | async-start | bytes 4194304 | tf_op jit(solution)/shard_map/all_to_all | solution.py:92
  17.5 51.1 %copy-start.27 = (s32[256,4]{0,1:T(4,128)S(1)}, s32[256,4]{0,1:T(4,128)}, u32[]{:S(2)}) copy-start(s32[256,4]{0,1:T(4,128)} %param.14) | copy-start | bytes 12292
  17.5 51.4 %copy-start.28 = (s32[256,4]{0,1:T(4,128)S(1)}, s32[256,4]{0,1:T(4,128)}, u32[]{:S(2)}) copy-start(s32[256,4]{0,1:T(4,128)} %param.13) | copy-start | bytes 12292
  17.5 52.4 %copy-start.31 = (f32[2,4]{1,0:T(2,128)S(1)}, f32[2,4]{1,0:T(2,128)}, u32[]{:S(2)}) copy-start(f32[2,4]{1,0:T(2,128)} %param.16) | copy-start | bytes 100
  17.5 52.5 %copy-start.29 = (s32[2,8,4]{1,2,0:T(4,128)S(1)}, s32[2,8,4]{1,2,0:T(4,128)}, u32[]{:S(2)}) copy-start(s32[2,8,4]{1,2,0:T(4,128)} %param.15) | copy-start | bytes 772
  17.5 52.5 %copy-start.30 = (f32[8]{0:T(128)S(1)}, f32[8]{0:T(128)}, u32[]{:S(2)}) copy-start(f32[8]{0:T(128)} %param.17) | copy-start | bytes 100
  65.0 53.4 %all-to-all-start = ((bf16[32,2,128,128]{3,2,1,0:T(8,128)(2,1)}), bf16[32,2,128,128]{3,2,1,0:T(8,128)(2,1)}, u32[]{:S(2)}, u32[]{:S(2)}) async-start(bf16[32,2,128,128]{3,2,1,0:T(8,128)(2,1)} %gather_fusion), calls=%async_computation | async-start | bytes 4194304 | tf_op jit(solution)/shard_map/all_to_all | solution.py:91
  73.4 48.8 %copy-start.16 = (bf16[32,2,128,128]{3,2,1,0:T(8,128)(2,1)S(1)}, bf16[32,2,128,128]{3,2,1,0:T(8,128)(2,1)}, u32[]{:S(2)}) copy-start(bf16[32,2,128,128]{3,2,1,0:T(8,128)(2,1)} %gather_fusion.3) | copy-start | bytes 6291460
  124.8 2.7 copy-start.3
  127.5 1.0 copy-start.14
  130.9 0.7 copy-start.4
  133.6 0.7 copy-start.5
  136.3 0.7 copy-start.7
  138.2 3.0 %copy-start.9 = (bf16[8,1,128,128]{2,3,1,0:T(8,128)(2,1)}, bf16[8,1,128,128]{2,3,1,0:T(8,128)(2,1)S(1)}, u32[]{:S(2)}) copy-start(bf16[8,1,128,128]{2,3,1,0:T(8,128)(2,1)S(1)} %fusion.64) | copy-start | bytes 786436
  139.1 2.2 copy-start.12
  141.3 52.9 %all-to-all-start.2 = ((bf16[32,2,128,128]{2,3,1,0:T(8,128)(2,1)}), bf16[32,2,128,128]{2,3,1,0:T(8,128)(2,1)S(1)}, u32[]{:S(2)}, u32[]{:S(2)}) async-start(bf16[32,2,128,128]{2,3,1,0:T(8,128)(2,1)} %gather_fusion.4), calls=%async_computation.2 | async-start | bytes 4194304 | tf_op jit(solution)/shard_map/all_to_all | solution.py:91
  194.1 1.3 copy-start.2
  195.5 52.9 %all-to-all-start.3 = ((bf16[32,2,128,128]{2,3,1,0:T(8,128)(2,1)}), bf16[32,2,128,128]{2,3,1,0:T(8,128)(2,1)S(1)}, u32[]{:S(2)}, u32[]{:S(2)}) async-start(bf16[32,2,128,128]{2,3,1,0:T(8,128)(2,1)} %gather_fusion.6), calls=%async_computation.3 | async-start | bytes 4194304 | tf_op jit(solution)/shard_map/all_to_all | solution.py:92
  198.4 3.1 %copy-start.6 = (bf16[8,1,128,128]{2,3,1,0:T(8,128)(2,1)S(1)}, bf16[8,1,128,128]{2,3,1,0:T(8,128)(2,1)}, u32[]{:S(2)}) copy-start(bf16[8,1,128,128]{2,3,1,0:T(8,128)(2,1)} %copy-done.5) | copy-start | bytes 786436
  198.5 4.5 %copy-start.24 = (bf16[8,1,128,128]{2,3,1,0:T(8,128)(2,1)S(1)}, bf16[8,1,128,128]{2,3,1,0:T(8,128)(2,1)}, u32[]{:S(2)}) copy-start(bf16[8,1,128,128]{2,3,1,0:T(8,128)(2,1)} %get-tuple-element.12) | copy-start | bytes 786436
  198.5 4.5 %copy-start.32 = (bf16[2,4,8,2,128,128]{5,4,3,2,1,0:T(8,128)(2,1)S(1)}, bf16[2,4,8,2,128,128]{5,4,3,2,1,0:T(8,128)(2,1)}, u32[]{:S(2)}) copy-start(bf16[2,4,8,2,128,128]{5,4,3,2,1,0:T(8,128)(2,1)} %param.10) | copy-start | bytes 12582916
  201.5 1.8 copy-start.8
  201.5 2.1 copy-start.25
  203.3 1.0 copy-start.10
  203.3 1.0 copy-start.13
  203.3 1.3 copy-start.26
  204.3 1.6 copy-start.11
  248.4 26.9 %all-to-all-start.4 = ((bf16[128,4,2,128]{3,2,1,0:T(2,128)(2,1)}), bf16[128,4,2,128]{3,2,1,0:T(2,128)(2,1)S(1)}, u32[]{:S(2)}, u32[]{:S(2)}) async-start(bf16[128,4,2,128]{3,2,1,0:T(2,128)(2,1)} %copy.307), calls=%async_computation.4 | async-start | bytes 524288 | tf_op jit(solution)/shard_map/all_to_all | solution.py:104
  256.2 2.3 copy-start.17
  257.2 1.3 copy-start.18
  258.5 2.9 %copy-start.19 = (bf16[8,1,2,128,128]{4,3,2,0,1:T(8,128)(2,1)S(1)}, bf16[8,1,2,128,128]{4,3,2,0,1:T(8,128)(2,1)}, u32[]{:S(2)}) copy-start(bf16[8,1,2,128,128]{4,3,2,0,1:T(8,128)(2,1)} %copy.391) | copy-start | bytes 1572868
  258.5 2.9 %copy-start.20 = (bf16[8,1,2,128,128]{4,3,2,0,1:T(8,128)(2,1)S(1)}, bf16[8,1,2,128,128]{4,3,2,0,1:T(8,128)(2,1)}, u32[]{:S(2)}) copy-start(bf16[8,1,2,128,128]{4,3,2,0,1:T(8,128)(2,1)} %copy.393) | copy-start | bytes 1572868
  258.5 2.9 %copy-start.21 = (bf16[8,1,2,128,128]{4,3,2,0,1:T(8,128)(2,1)S(1)}, bf16[8,1,2,128,128]{4,3,2,0,1:T(8,128)(2,1)}, u32[]{:S(2)}) copy-start(bf16[8,1,2,128,128]{4,3,2,0,1:T(8,128)(2,1)} %copy.394) | copy-start | bytes 1572868
  258.6 2.9 %copy-start.22 = (bf16[8,1,2,128,128]{4,3,2,0,1:T(8,128)(2,1)S(1)}, bf16[8,1,2,128,128]{4,3,2,0,1:T(8,128)(2,1)}, u32[]{:S(2)}) copy-start(bf16[8,1,2,128,128]{4,3,2,0,1:T(8,128)(2,1)} %copy.396) | copy-start | bytes 1572868
  258.6 2.9 %copy-start.23 = (bf16[8,1,2,128,128]{4,3,2,0,1:T(8,128)(2,1)S(1)}, bf16[8,1,2,128,128]{4,3,2,0,1:T(8,128)(2,1)}, u32[]{:S(2)}) copy-start(bf16[8,1,2,128,128]{4,3,2,0,1:T(8,128)(2,1)} %copy.395) | copy-start | bytes 1572868
  262.6 1.0 copy-start.15
  264.8 2.2 copy-start.33
  275.3 16.3 %all-to-all-start.5 = ((bf16[128,4,2,128]{3,2,1,0:T(2,128)(2,1)}), bf16[128,4,2,128]{3,2,1,0:T(2,128)(2,1)S(1)}, u32[]{:S(2)}, u32[]{:S(2)}) async-start(bf16[128,4,2,128]{3,2,1,0:T(2,128)(2,1)} %copy.309), calls=%async_computation.5 | async-start | bytes 524288 | tf_op jit(solution)/shard_map/all_to_all | solution.py:104

commit v2 on v1

v2 whole, which is shorter than its diff:
```python
import functools

import jax
import jax.numpy as jnp
from jax import lax
from jax.experimental import pallas as pl
from jax.experimental.pallas import tpu as pltpu
from jax.sharding import PartitionSpec as P

MESH = pl.DeviceIdType.MESH
F32 = jnp.float32
BF16 = jnp.bfloat16


def dot(a, b):
    return jnp.dot(a, b, preferred_element_type=F32)


def kernel(
    dims,
    picks,
    takes,
    weights,
    decay,
    adjoint,
    saved,
    propagators,
    coupling,
    out,
    terms,
    right_u,
    left_u,
    hist,
    stage,
    inbox,
    *rest,
):
    nodes, depth, width, count, modes, steps, subs, dim = dims
    hops = depth - 1
    chain = rest[: 2 * steps * hops]
    chain_send, chain_recv, plane_send, plane_recv, credit = rest[2 * steps * hops :]
    cores = depth * width
    owners = nodes * cores
    lanes = nodes * width
    node = lax.axis_index("node")
    spot = lax.axis_index("cores")
    level = spot // width
    column = spot % width
    lane = node * width + column

    def lane_of(offset):
        return lax.rem(lane + offset, lanes)

    def lane_id(other):
        return (other // width, level * width + other % width)

    def level_id(other):
        return (node, other * width + column)

    def owner_of(a_lane, a_level):
        return (a_lane // width) * cores + a_level * width + a_lane % width

    barrier = pltpu.get_barrier_semaphore()

    def greet(offset, carry):
        pl.semaphore_signal(
            barrier, inc=1, device_id=lane_id(lane_of(offset)), device_id_type=MESH
        )
        return carry

    lax.fori_loop(1, lanes, greet, 0)

    @pl.when(level > 0)
    def _():
        pl.semaphore_signal(barrier, inc=1, device_id=level_id(level - 1), device_id_type=MESH)

    @pl.when(level < depth - 1)
    def _():
        pl.semaphore_signal(barrier, inc=1, device_id=level_id(level + 1), device_id_type=MESH)

    inner = jnp.where(level > 0, 1, 0) + jnp.where(level < depth - 1, 1, 0)
    pl.semaphore_wait(barrier, lanes - 1 + inner)

    def chain_block(step, way, hop):
        return chain[(step * 2 + way) * hops + hop - 1]

    def chain_copy(step, way, hop, source):
        peer = level + 1 if way == 0 else level - 1
        return pltpu.make_async_remote_copy(
            src_ref=source,
            dst_ref=chain_block(step, way, hop),
            send_sem=chain_send.at[step, way, hop - 1],
            recv_sem=chain_recv.at[step, way, hop - 1],
            device_id=level_id(peer),
            device_id_type=MESH,
        )

    def from_level(way, hop):
        return level - hop if way == 0 else level + hop

    def arrives(way, hop):
        return level >= hop if way == 0 else level + hop < depth

    def goes_on(way, hop):
        if way == 0:
            return jnp.logical_and(level >= hop - 1, level < depth - 1)
        return jnp.logical_and(level + hop - 1 < depth, level > 0)

    def plane_copy(offset, a_level):
        return pltpu.make_async_remote_copy(
            src_ref=stage.at[offset - 1, a_level],
            dst_ref=inbox.at[owner_of(lane, a_level)],
            send_sem=plane_send.at[offset - 1, a_level],
            recv_sem=plane_recv.at[owner_of(lane, a_level)],
            device_id=lane_id(lane_of(offset)),
            device_id_type=MESH,
        )

    def serve(block, a_level):
        source = owner_of(lane, a_level)

        def pick(offset, way):
            target = owner_of(lane_of(offset), level)
            return picks[(way * owners + target) * owners + source]

        for way in range(2):
            inbox[source, way] = block[pick(0, way)]

        def fill(offset, carry):
            for way in range(2):
                stage[offset - 1, a_level, way] = block[pick(offset, way)]
            return carry

        lax.fori_loop(1, lanes, fill, 0)

        def send(offset, carry):
            plane_copy(offset, a_level).start()
            return carry

        lax.fori_loop(1, lanes, send, 0)

    def prepare():
        def one(at, carry):
            step, sub = at // subs, at % subs
            u_re = propagators[step, sub, 0]
            u_im = propagators[step, sub, 1]
            right_u[at, :dim, :dim] = u_re
            right_u[at, :dim, dim:] = u_im
            right_u[at, dim:, :dim] = -u_im
            right_u[at, dim:, dim:] = u_re
            t_re = u_re.T
            t_im = u_im.T
            left_u[at, :dim, :dim] = t_re
            left_u[at, :dim, dim:] = t_im
            left_u[at, dim:, :dim] = -t_im
            left_u[at, dim:, dim:] = t_re
            return carry

        lax.fori_loop(0, steps * subs, one, 0)

    def project(step):
        def one(sub, carry):
            total = jnp.zeros((dim, 2 * dim), F32)
            for j in range(count):
                kept = saved[step, sub, j].reshape(2 * dim, dim)
                lam_re = hist[step, sub + 1, j, 0]
                lam_im = hist[step, sub + 1, j, 1]
                both = jnp.concatenate(
                    [
                        jnp.concatenate([lam_re, lam_im], axis=1),
                        jnp.concatenate([lam_im, -lam_re], axis=1),
                    ],
                    axis=0,
                )
                total = total + lax.dot_general(
                    kept, both, (((0,), (0,)), ((), ())), preferred_element_type=F32
                )
            terms[step * subs + sub] = total.astype(BF16)
            return carry

        lax.fori_loop(0, subs, one, 0)

    def couple(step, state):
        operator = coupling[...]

        def one(j, carry):
            plus, minus = [], []
            for part in range(2):
                sums = []
                for way in range(2):
                    total = jnp.zeros((dim, dim), F32)
                    for mode in range(modes):
                        at = (way * count + j) * modes + mode
                        total = total + weights[at] * inbox[takes[at], way, part].astype(F32)
                    sums.append(total)
                plus.append((sums[0] + sums[1]).astype(BF16))
                minus.append((sums[0] - sums[1]).astype(BF16))
            left = dot(operator, jnp.concatenate([plus[1], -plus[0]], axis=1))
            right = dot(jnp.concatenate([minus[1], -minus[0]], axis=0), operator)
            for part in range(2):
                lam = decay[j] * state[j, part].astype(F32)
                lam = lam + left[:, part * dim : (part + 1) * dim]
                lam = lam - right[part * dim : (part + 1) * dim]
                hist[step, 0, j, part] = lam.astype(BF16)
            return carry

        lax.fori_loop(0, count, one, 0)

    def rotate(step):
        def one(sub, carry):
            at = step * subs + sub
            mult_r = right_u[at]
            mult_l = left_u[at]
            for j in range(0, count, 2):
                rows = jnp.concatenate(
                    [
                        jnp.concatenate(
                            [hist[step, sub, j + i, 0], hist[step, sub, j + i, 1]], axis=1
                        )
                        for i in range(2)
                    ],
                    axis=0,
                )
                middle = dot(rows, mult_r).astype(BF16)
                stacked = jnp.concatenate(
                    [
                        jnp.concatenate([middle[:dim, :dim], middle[dim:, :dim]], axis=1),
                        jnp.concatenate([middle[:dim, dim:], middle[dim:, dim:]], axis=1),
                    ],
                    axis=0,
                )
                result = dot(mult_l, stacked).astype(BF16)
                for i in range(2):
                    for part in range(2):
                        hist[step, sub + 1, j + i, part] = result[
                            part * dim : (part + 1) * dim, i * dim : (i + 1) * dim
                        ]
            return carry

        lax.fori_loop(0, subs, one, 0)

    for step in range(steps):
        state = adjoint if step == 0 else hist.at[step - 1, subs]
        for way in range(2):

            @pl.when(goes_on(way, 1))
            def _(way=way):
                chain_copy(step, way, 1, state).start()

        if step > 0:
            pl.semaphore_wait(credit, lanes - 1)
        serve(state, level)
        if step == 0:
            prepare()
        else:
            project(step - 1)
        for hop in range(1, depth):
            for way in range(2):

                @pl.when(arrives(way, hop))
                def _(way=way, hop=hop):
                    block = chain_block(step, way, hop)
                    chain_copy(step, way, hop, block).wait_recv()
                    if hop + 1 < depth:

                        @pl.when(goes_on(way, hop + 1))
                        def _():
                            chain_copy(step, way, hop + 1, block).start()

                    serve(block, from_level(way, hop))

        def collect(offset, carry):
            for a_level in range(depth):
                source = owner_of(lane_of(offset), a_level)
                pltpu.make_async_remote_copy(
                    src_ref=stage.at[offset - 1, a_level],
                    dst_ref=inbox.at[source],
                    send_sem=plane_send.at[offset - 1, a_level],
                    recv_sem=plane_recv.at[source],
                    device_id=lane_id(lane_of(offset)),
                    device_id_type=MESH,
                ).wait_recv()
            return carry

        lax.fori_loop(1, lanes, collect, 0)
        couple(step, state)
        if step + 1 < steps:

            def allow(offset, carry):
                pl.semaphore_signal(
                    credit, inc=1, device_id=lane_id(lane_of(offset)), device_id_type=MESH
                )
                return carry

            lax.fori_loop(1, lanes, allow, 0)
        rotate(step)

        def settle(offset, carry):
            for a_level in range(depth):
                plane_copy(offset, a_level).wait_send()
            return carry

        lax.fori_loop(1, lanes, settle, 0)
        for hop in range(1, depth):
            for way in range(2):

                @pl.when(goes_on(way, hop))
                def _(way=way, hop=hop):
                    chain_copy(step, way, hop, chain_block(step, way, hop)).wait_send()

    out[...] = hist[steps - 1, subs]
    project(steps - 1)


def pick_table(links, owners, count):
    flat = links.reshape(owners, -1)
    hit = (flat // count)[:, None, :] == jnp.arange(owners)[None, :, None]
    return jnp.sum(jnp.where(hit, (flat % count)[:, None, :], 0), axis=2).reshape(-1)


def body(adjoint, saved, propagators, coupling, higher, lower, ladder, rates, decay):
    nodes = lax.axis_size("node")
    cores = lax.axis_size("cores")
    owners = nodes * cores
    own = lax.axis_index(("node", "cores"))
    count = adjoint.shape[0]
    modes = higher.shape[1]
    steps, subs = propagators.shape[:2]
    dim = coupling.shape[0]
    depth = 1 << (cores.bit_length() // 2)
    width = cores // depth
    lanes = nodes * width
    grad_rows = dim // owners if dim >= owners else 1
    picks = jnp.concatenate(
        [pick_table(higher, owners, count), pick_table(lower, owners, count)]
    ).astype(jnp.int32)
    own_links = lax.dynamic_slice_in_dim(jnp.stack([higher, lower]), own * count, count, 1)
    takes = (own_links // count).reshape(-1).astype(jnp.int32)
    weights = (ladder.astype(F32) * rates[:, None, :]).reshape(-1)
    block = adjoint.shape
    smem = pl.BlockSpec(memory_space=pltpu.SMEM)
    vmem = pl.BlockSpec(memory_space=pltpu.VMEM)
    hops = depth - 1
    state, terms = pl.pallas_call(
        functools.partial(kernel, (nodes, depth, width, count, modes, steps, subs, dim)),
        out_shape=(
            jax.ShapeDtypeStruct(block, BF16),
            jax.ShapeDtypeStruct((steps * subs, dim, 2 * dim), BF16),
        ),
        in_specs=[smem] * 4 + [vmem] * 4,
        out_specs=(vmem, vmem),
        scratch_shapes=[
            pltpu.VMEM((steps * subs, 2 * dim, 2 * dim), BF16),
            pltpu.VMEM((steps * subs, 2 * dim, 2 * dim), BF16),
            pltpu.VMEM((steps, subs + 1) + block, BF16),
            pltpu.VMEM((lanes - 1, depth, 2) + block[1:], BF16),
            pltpu.VMEM((owners, 2) + block[1:], BF16),
            *[pltpu.VMEM(block, BF16) for _ in range(2 * steps * hops)],
            pltpu.SemaphoreType.DMA((steps, 2, hops)),
            pltpu.SemaphoreType.DMA((steps, 2, hops)),
            pltpu.SemaphoreType.DMA((lanes - 1, depth)),
            pltpu.SemaphoreType.DMA((owners,)),
            pltpu.SemaphoreType.REGULAR,
        ],
        compiler_params=pltpu.CompilerParams(
            collective_id=0, has_side_effects=True, vmem_limit_bytes=63_000_000
        ),
    )(picks, takes, weights, decay, adjoint, saved, propagators, coupling)
    swapped = lax.all_to_all(
        jnp.swapaxes(terms, 0, 1), ("node", "cores"), split_axis=0, concat_axis=0, tiled=True
    )
    by_owner = swapped.reshape(owners, grad_rows, steps * subs, 2, dim)
    gradient = jnp.sum(by_owner.astype(F32), axis=0)
    return state, gradient


def solution(mesh):
    return jax.shard_map(
        body,
        mesh=mesh,
        in_specs=(
            P(("node", "cores"), None, None, None),
            P(None, None, ("node", "cores"), None, None, None),
            P(),
            P(),
            P(),
            P(),
            P(None, ("node", "cores"), None),
            P(),
            P(("node", "cores")),
        ),
        out_specs=(P(("node", "cores"), None, None, None), P(("node", "cores"), None, None, None)),
        check_vma=False,
    )
```

time: 294 us -> 154 us (0.52)
  waiting for transfers between devices: 176 us -> 16.2 us
  Pallas kernels: 0 us -> 120 us
  local copies, waits for them, and re-layouts: 49.7 us -> 8.08 us
  matrix products: 28 us -> 0 us
  starting transfers between devices: 25.7 us -> 4.39 us
  other arithmetic: 11.2 us -> 3.52 us
    all_to_all x6 -> x1, waiting for transfers between devices: 176 us -> 16.2 us  [body(): lax.all_to_all(jnp.swapaxes(terms, 0, 1), ('node', 'cores'), split_axis=0...]
    pallas_call x0 -> x1, Pallas kernels: none -> 120 us  [body(): pl.pallas_call(functools.partial(kernel, (nodes, depth, width, count, mod...]
    dot_general x52 -> x0, matrix products: 28 us -> none  [the longest x2 5.43 us: couple_step(): jnp.einsum('jxab,bc->jxac', minus, coupling, preferred_element_type=jnp.f...]
    all_to_all x6 -> x1, starting transfers between devices: 25.7 us -> 4.39 us  [body(): lax.all_to_all(jnp.swapaxes(terms, 0, 1), ('node', 'cores'), split_axis=0...]
    gather x8 -> x0, local copies, waits for them, and re-layouts: 20.5 us -> none  [the longest x4 11.9 us: linked_sum(): chosen = received[picks].reshape((own_count, modes) + received.shape[1:])]
    unnamed x81 -> x4, local copies, waits for them, and re-layouts: 21.3 us -> 4.15 us
    slice x2 -> x0, local copies, waits for them, and re-layouts: 4.55 us -> none  [linked_sum(): total = factors[:, 0, None, None, None] * chosen[:, 0].astype(jnp.float32)]
    neg x8 -> x0, other arithmetic: 3.68 us -> none  [projection(): swapped = jnp.stack([state[:, 1], -state[:, 0]], axis=1)]
  transfers between devices with their start and end apart: 6 -> 1, of which waited for: 5 -> 1; matrix products, arithmetic and copies ran while one was open for 19% -> 0% of each run, Pallas kernels for 0% -> 0%
where the time goes in v2:
time: 154 us; the launch traced here: 153 us
  Pallas kernels  120 us (78%)
  waiting for transfers between devices  16.2 us (11%)
  local copies, waits for them, and re-layouts  8.08 us (5%)
  starting transfers between devices  4.39 us (3%)
  other arithmetic  3.52 us (2%)
    pallas_call x1, Pallas kernels, body(): pl.pallas_call(functools.partial(kernel, (nodes, depth, width, count, mod...  120 us
    all_to_all x1, waiting for transfers between devices, body(): lax.all_to_all(jnp.swapaxes(terms, 0, 1), ('node', 'cores'), split_axis=0...  16.2 us
    all_to_all x1, starting transfers between devices, body(): lax.all_to_all(jnp.swapaxes(terms, 0, 1), ('node', 'cores'), split_axis=0...  4.39 us
    unnamed x4, local copies, waits for them, and re-layouts  4.15 us
  transfers between devices with their start and end apart: 1, of which 1 were waited for; matrix products, arithmetic and copies ran while one was open for 0% of the time, Pallas kernels for 0%

profile of v2, /device:TPU:0, one launch (start us, length us, event | category | flops | bytes accessed | tf_op | source)
XLA Modules:
  0.0 153.3 jit_solution(14288742144388847232)
XLA Ops:
  0.6 0.8 copy.24
  1.5 0.8 copy.25
  2.3 0.8 add_select_fusion.4
  3.1 0.1 copy.26
  3.2 0.6 reshape.128.takes
  3.8 0.8 convert_multiply_fusion
  4.5 0.1 copy.27
  4.6 0.7 reshape.129.weights
  5.3 0.1 reshape.124
  5.4 0.6 select_reduce_fusion.1
  6.1 0.1 reshape.125
  6.1 0.1 reshape.126
  6.3 0.6 select_reduce_fusion
  6.9 0.1 reshape.127
  7.0 0.6 pad_add_fusion.picks
  7.6 120.4 %shard_map.104 = (bf16[8,2,128,128]{3,2,1,0:T(8,128)(2,1)}, bf16[8,128,256]{2,1,0:T(8,128)(2,1)}) custom-call(s32[2048]{0:T(1024)} %pad_add_fusion.picks, s32[64]{0:T(128)} %reshape.128.takes, f32[64]{0:T(128)} %reshape.129.weights, f32[8]{0:T(128)} %decay.1, bf16[8,2,128,128]{3,2,1,0:T(8,128)(2,1)} %adjoint.1, bf16[2,4,8,2,128,128]{5,4,3,2,1,0:T(8,128)(2,1)} %saved.1, ...), custom_call_target="tpu_custom_call" | custom-call | tf_op jit(solution)/shard_map/pallas_call | solution.py:344
  127.9 2.1 %copy.28 = bf16[128,8,256]{2,1,0:T(8,128)(2,1)} copy(bf16[128,8,256]{2,0,1:T(8,128)(2,1)} %bitcast.6) | data formatting | bytes 1048576 | tf_op jit(solution)/shard_map/transpose | solution.py:370
  130.1 4.4 %all-to-all-start = ((bf16[128,8,256]{2,1,0:T(8,128)(2,1)}), bf16[128,8,256]{2,1,0:T(8,128)(2,1)S(1)}, u32[]{:S(2)}, u32[]{:S(2)}) async-start(bf16[128,8,256]{2,1,0:T(8,128)(2,1)} %copy.28), calls=%async_computation | async-start | bytes 1048576 | tf_op jit(solution)/shard_map/all_to_all | solution.py:369
  134.5 16.2 %all-to-all-done = bf16[128,8,256]{2,1,0:T(8,128)(2,1)S(1)} async-done(((bf16[128,8,256]{2,1,0:T(8,128)(2,1)}), bf16[128,8,256]{2,1,0:T(8,128)(2,1)S(1)}, u32[]{:S(2)}, u32[]{:S(2)}) %all-to-all-start) | async-done | bytes 524320 | tf_op jit(solution)/shard_map/all_to_all | solution.py:369
  150.7 0.1 convert_reduce_fusion
  150.8 0.6 copy.30
  151.4 1.9 %copy.34 = bf16[8,2,128,128]{3,2,1,0:T(8,128)(2,1)} copy(bf16[8,2,128,128]{3,2,1,0:T(8,128)(2,1)} %get-tuple-element.16) | data formatting | bytes 1048576
  (2 shorter events, 0.0 us)
Async XLA Ops:
  130.1 20.6 %all-to-all-start = ((bf16[128,8,256]{2,1,0:T(8,128)(2,1)}), bf16[128,8,256]{2,1,0:T(8,128)(2,1)S(1)}, u32[]{:S(2)}, u32[]{:S(2)}) async-start(bf16[128,8,256]{2,1,0:T(8,128)(2,1)} %copy.28), calls=%async_computation | async-start | bytes 1048576 | tf_op jit(solution)/shard_map/all_to_all | solution.py:369

commit v3 on v2

--- a/solution.py
+++ b/solution.py
@@ -19,29 +19,38 @@
 def kernel(
     dims,
     picks,
-    takes,
-    weights,
+    higher,
+    lower,
+    ladder,
+    rates,
     decay,
     adjoint,
     saved,
     propagators,
     coupling,
     out,
-    terms,
+    grad,
     right_u,
     left_u,
     hist,
     stage,
     inbox,
+    terms,
+    term_stage,
+    term_inbox,
     *rest,
 ):
-    nodes, depth, width, count, modes, steps, subs, dim = dims
+    nodes, depth, width, count, modes, steps, subs, dim, halves = dims
     hops = depth - 1
     chain = rest[: 2 * steps * hops]
-    chain_send, chain_recv, plane_send, plane_recv, credit = rest[2 * steps * hops :]
+    chain_send, chain_recv, plane_send, plane_recv, term_send, term_recv, credit = rest[
+        2 * steps * hops :
+    ]
     cores = depth * width
     owners = nodes * cores
     lanes = nodes * width
+    rows = dim // owners
+    batch = subs // halves
     node = lax.axis_index("node")
     spot = lax.axis_index("cores")
     level = spot // width
@@ -62,24 +71,18 @@
 
     barrier = pltpu.get_barrier_semaphore()
 
+    own = node * cores + spot
+
+    def owner_id(offset):
+        other = lax.rem(own + offset, owners)
+        return (other // cores, lax.rem(other, cores))
+
     def greet(offset, carry):
-        pl.semaphore_signal(
-            barrier, inc=1, device_id=lane_id(lane_of(offset)), device_id_type=MESH
-        )
+        pl.semaphore_signal(barrier, inc=1, device_id=owner_id(offset), device_id_type=MESH)
         return carry
 
-    lax.fori_loop(1, lanes, greet, 0)
-
-    @pl.when(level > 0)
-    def _():
-        pl.semaphore_signal(barrier, inc=1, device_id=level_id(level - 1), device_id_type=MESH)
-
-    @pl.when(level < depth - 1)
-    def _():
-        pl.semaphore_signal(barrier, inc=1, device_id=level_id(level + 1), device_id_type=MESH)
-
-    inner = jnp.where(level > 0, 1, 0) + jnp.where(level < depth - 1, 1, 0)
-    pl.semaphore_wait(barrier, lanes - 1 + inner)
+    lax.fori_loop(1, owners, greet, 0)
+    pl.semaphore_wait(barrier, owners - 1)
 
     def chain_block(step, way, hop):
         return chain[(step * 2 + way) * hops + hop - 1]
@@ -121,7 +124,7 @@
 
         def pick(offset, way):
             target = owner_of(lane_of(offset), level)
-            return picks[(way * owners + target) * owners + source]
+            return picks[way * owners + source, target]
 
         for way in range(2):
             inbox[source, way] = block[pick(0, way)]
@@ -158,8 +161,11 @@
 
         lax.fori_loop(0, steps * subs, one, 0)
 
-    def project(step):
-        def one(sub, carry):
+    def project(step, half):
+        group = step * halves + half
+
+        def one(place, carry):
+            sub = half * batch + place
             total = jnp.zeros((dim, 2 * dim), F32)
             for j in range(count):
                 kept = saved[step, sub, j].reshape(2 * dim, dim)
@@ -175,10 +181,37 @@
                 total = total + lax.dot_general(
                     kept, both, (((0,), (0,)), ((), ())), preferred_element_type=F32
                 )
-            terms[step * subs + sub] = total.astype(BF16)
-            return carry
-
-        lax.fori_loop(0, subs, one, 0)
+            terms[place] = total
+            return carry
+
+        lax.fori_loop(0, batch, one, 0)
+        for target in range(owners):
+            term_stage[group, target] = jnp.concatenate(
+                [terms[i, target * rows : (target + 1) * rows] for i in range(batch)], axis=0
+            ).astype(BF16)
+
+        def send(offset, carry):
+            pltpu.make_async_remote_copy(
+                src_ref=term_stage.at[group, lax.rem(own + offset, owners)],
+                dst_ref=term_inbox.at[group, offset - 1],
+                send_sem=term_send.at[group],
+                recv_sem=term_recv.at[group],
+                device_id=owner_id(offset),
+                device_id_type=MESH,
+            ).start()
+            return carry
+
+        lax.fori_loop(1, owners, send, 0)
+
+    def finish(group):
+        everything = term_inbox.at[group]
+        pltpu.make_async_copy(everything, everything, term_recv.at[group]).wait()
+        total = term_stage[group, own].astype(F32)
+        for offset in range(1, owners):
+            total = total + term_inbox[group, offset - 1].astype(F32)
+        for i in range(batch):
+            grad[group * batch + i] = total[i * rows : (i + 1) * rows]
+        pltpu.make_async_copy(everything, everything, term_send.at[group]).wait()
 
     def couple(step, state):
         operator = coupling[...]
@@ -190,8 +223,9 @@
                 for way in range(2):
                     total = jnp.zeros((dim, dim), F32)
                     for mode in range(modes):
-                        at = (way * count + j) * modes + mode
-                        total = total + weights[at] * inbox[takes[at], way, part].astype(F32)
+                        weight = ladder[way, mode, j].astype(F32) * rates[way, mode]
+                        place = lax.div((higher, lower)[way][mode, own * count + j], count)
+                        total = total + weight * inbox[place, way, part].astype(F32)
                     sums.append(total)
                 plus.append((sums[0] + sums[1]).astype(BF16))
                 minus.append((sums[0] - sums[1]).astype(BF16))
@@ -206,7 +240,7 @@
 
         lax.fori_loop(0, count, one, 0)
 
-    def rotate(step):
+    def rotate(step, half):
         def one(sub, carry):
             at = step * subs + sub
             mult_r = right_u[at]
@@ -237,7 +271,7 @@
                         ]
             return carry
 
-        lax.fori_loop(0, subs, one, 0)
+        lax.fori_loop(half * batch, (half + 1) * batch, one, 0)
 
     for step in range(steps):
         state = adjoint if step == 0 else hist.at[step - 1, subs]
@@ -253,7 +287,8 @@
         if step == 0:
             prepare()
         else:
-            project(step - 1)
+            for half in range(halves):
+                project(step - 1, half)
         for hop in range(1, depth):
             for way in range(2):
 
@@ -293,7 +328,10 @@
                 return carry
 
             lax.fori_loop(1, lanes, allow, 0)
-        rotate(step)
+        for half in range(halves):
+            rotate(step, half)
+            if step == steps - 1:
+                project(step, half)
 
         def settle(offset, carry):
             for a_level in range(depth):
@@ -309,13 +347,24 @@
                     chain_copy(step, way, hop, chain_block(step, way, hop)).wait_send()
 
     out[...] = hist[steps - 1, subs]
-    project(steps - 1)
-
-
-def pick_table(links, owners, count):
-    flat = links.reshape(owners, -1)
-    hit = (flat // count)[:, None, :] == jnp.arange(owners)[None, :, None]
-    return jnp.sum(jnp.where(hit, (flat % count)[:, None, :], 0), axis=2).reshape(-1)
+    for group in range(steps * halves):
+        finish(group)
+
+
+def pick_kernel(owners, count, modes, higher, lower, picks):
+    total = owners * count
+    names = lax.broadcasted_iota(jnp.int32, (owners, total), 0)
+    member = lax.div(lax.broadcasted_iota(jnp.int32, (total, owners), 0), count)
+    member = (member == lax.broadcasted_iota(jnp.int32, (total, owners), 1)).astype(F32)
+    for way, table in enumerate((higher, lower)):
+        spread = jnp.zeros((owners, total), F32)
+        for mode in range(modes):
+            link = table[mode : mode + 1, :]
+            source = lax.div(link, count)
+            local = (link - source * count).astype(F32)
+            spread = spread + jnp.where(source == names, local, 0.0)
+        found = dot(spread.astype(BF16), member.astype(BF16))
+        picks[way * owners : (way + 1) * owners, :] = found.astype(jnp.int32)
 
 
 def body(adjoint, saved, propagators, coupling, higher, lower, ladder, rates, decay):
@@ -330,24 +379,27 @@
     depth = 1 << (cores.bit_length() // 2)
     width = cores // depth
     lanes = nodes * width
-    grad_rows = dim // owners if dim >= owners else 1
-    picks = jnp.concatenate(
-        [pick_table(higher, owners, count), pick_table(lower, owners, count)]
-    ).astype(jnp.int32)
-    own_links = lax.dynamic_slice_in_dim(jnp.stack([higher, lower]), own * count, count, 1)
-    takes = (own_links // count).reshape(-1).astype(jnp.int32)
-    weights = (ladder.astype(F32) * rates[:, None, :]).reshape(-1)
-    block = adjoint.shape
+    rows = dim // owners
+    halves = 2 if subs % 2 == 0 else 1
+    batch = subs // halves
+    higher, lower, ladder = higher.T, lower.T, jnp.swapaxes(ladder, 1, 2)
     smem = pl.BlockSpec(memory_space=pltpu.SMEM)
     vmem = pl.BlockSpec(memory_space=pltpu.VMEM)
+    picks = pl.pallas_call(
+        functools.partial(pick_kernel, owners, count, modes),
+        out_shape=jax.ShapeDtypeStruct((2 * owners, owners), jnp.int32),
+        in_specs=[vmem, vmem],
+        out_specs=vmem,
+    )(higher, lower)
+    block = adjoint.shape
     hops = depth - 1
-    state, terms = pl.pallas_call(
-        functools.partial(kernel, (nodes, depth, width, count, modes, steps, subs, dim)),
+    state, grad = pl.pallas_call(
+        functools.partial(kernel, (nodes, depth, width, count, modes, steps, subs, dim, halves)),
         out_shape=(
             jax.ShapeDtypeStruct(block, BF16),
-            jax.ShapeDtypeStruct((steps * subs, dim, 2 * dim), BF16),
+            jax.ShapeDtypeStruct((steps * subs, rows, 2 * dim), F32),
         ),
-        in_specs=[smem] * 4 + [vmem] * 4,
+        in_specs=[smem] * 6 + [vmem] * 4,
         out_specs=(vmem, vmem),
         scratch_shapes=[
             pltpu.VMEM((steps * subs, 2 * dim, 2 * dim), BF16),
@@ -355,22 +407,23 @@
             pltpu.VMEM((steps, subs + 1) + block, BF16),
             pltpu.VMEM((lanes - 1, depth, 2) + block[1:], BF16),
             pltpu.VMEM((owners, 2) + block[1:], BF16),
+            pltpu.VMEM((batch, dim, 2 * dim), F32),
+            pltpu.VMEM((steps * halves, owners, batch * rows, 2 * dim), BF16),
+            pltpu.VMEM((steps * halves, owners - 1, batch * rows, 2 * dim), BF16),
             *[pltpu.VMEM(block, BF16) for _ in range(2 * steps * hops)],
             pltpu.SemaphoreType.DMA((steps, 2, hops)),
             pltpu.SemaphoreType.DMA((steps, 2, hops)),
             pltpu.SemaphoreType.DMA((lanes - 1, depth)),
             pltpu.SemaphoreType.DMA((owners,)),
+            pltpu.SemaphoreType.DMA((steps * halves,)),
+            pltpu.SemaphoreType.DMA((steps * halves,)),
             pltpu.SemaphoreType.REGULAR,
         ],
         compiler_params=pltpu.CompilerParams(
             collective_id=0, has_side_effects=True, vmem_limit_bytes=63_000_000
         ),
-    )(picks, takes, weights, decay, adjoint, saved, propagators, coupling)
-    swapped = lax.all_to_all(
-        jnp.swapaxes(terms, 0, 1), ("node", "cores"), split_axis=0, concat_axis=0, tiled=True
-    )
-    by_owner = swapped.reshape(owners, grad_rows, steps * subs, 2, dim)
-    gradient = jnp.sum(by_owner.astype(F32), axis=0)
+    )(picks, higher, lower, ladder, rates, decay, adjoint, saved, propagators, coupling)
+    gradient = jnp.swapaxes(grad, 0, 1).reshape(rows, steps * subs, 2, dim)
     return state, gradient
 
 

time: 154 us -> 138 us (0.90)
  waiting for transfers between devices: 16.2 us -> 0 us
  Pallas kernels: 120 us -> 134 us
  local copies, waits for them, and re-layouts: 8.08 us -> 3.3 us
  starting transfers between devices: 4.39 us -> 0 us
  other arithmetic: 3.52 us -> 0 us
    all_to_all x1 -> x0, waiting for transfers between devices: 16.2 us -> none  [body(): lax.all_to_all(jnp.swapaxes(terms, 0, 1), ('node', 'cores'), split_axis=0...]
    pallas_call x1, Pallas kernels: 120 us -> 132 us  [body(): pl.pallas_call(functools.partial(kernel, (nodes, depth, width, count, mod...]
    all_to_all x1 -> x0, starting transfers between devices: 4.39 us -> none  [body(): lax.all_to_all(jnp.swapaxes(terms, 0, 1), ('node', 'cores'), split_axis=0...]
    transpose x1 -> x0, local copies, waits for them, and re-layouts: 2.13 us -> none  [body(): jnp.swapaxes(terms, 0, 1)]
    unnamed x4 -> x2, local copies, waits for them, and re-layouts: 4.15 us -> 2.51 us
  transfers between devices with their start and end apart: 1 -> 0, of which waited for: 1 -> 0; matrix products, arithmetic and copies ran while one was open for 0% -> 0% of each run, Pallas kernels for 0% -> 0%
where the time goes in v3:
time: 138 us
  Pallas kernels  134 us (97%)
  local copies, waits for them, and re-layouts  3.3 us (2%)
    pallas_call x1, Pallas kernels, body(): pl.pallas_call(functools.partial(kernel, (nodes, depth, width, count, mod...  132 us

profile of v3, /device:TPU:0, one launch (start us, length us, event | category | flops | bytes accessed | tf_op | source)
XLA Modules:
  0.0 137.6 jit_solution(11845028885761188782)
XLA Ops:
  0.6 1.5 %shard_map.104.picks = s32[64,32]{1,0:T(8,128)} custom-call(s32[4,256]{1,0:T(4,128)} %bitcast.7, s32[4,256]{1,0:T(4,128)} %bitcast.9), custom_call_target="tpu_custom_call" | custom-call | tf_op jit(solution)/shard_map/pallas_call | solution.py:388
  2.1 132.2 %shard_map.105 = (bf16[8,2,128,128]{3,2,1,0:T(8,128)(2,1)}, f32[8,4,256]{2,1,0:T(4,128)}) custom-call(s32[64,32]{1,0:T(8,128)} %shard_map.104.picks, s32[4,256]{1,0:T(4,128)} %bitcast.8, s32[4,256]{1,0:T(4,128)} %bitcast.10, s32[2,4,8]{2,1,0:T(4,128)} %bitcast.11, f32[2,4]{1,0:T(2,128)} %rates.1, f32[8]{0:T(128)} %decay.1, bf16[8,2,128,128]{3,2,1,0:T(8,128)(2,1)} %adjoint.1, ...), custom_call_target="tpu_custom_call" | custom-call | tf_op jit(solution)/shard_map/pallas_call | solution.py:396
  134.3 0.8 reshape.7
  135.1 0.6 copy.11
  135.7 1.9 %copy.13 = bf16[8,2,128,128]{3,2,1,0:T(8,128)(2,1)} copy(bf16[8,2,128,128]{3,2,1,0:T(8,128)(2,1)} %get-tuple-element.10) | data formatting | bytes 1048576

commit v4 on v3

--- a/solution.py
+++ b/solution.py
@@ -25,7 +25,7 @@
     rates,
     decay,
     adjoint,
-    saved,
+    saved_in,
     propagators,
     coupling,
     out,
@@ -38,12 +38,14 @@
     terms,
     term_stage,
     term_inbox,
+    saved,
+    saved_t,
     *rest,
 ):
     nodes, depth, width, count, modes, steps, subs, dim, halves = dims
     hops = depth - 1
     chain = rest[: 2 * steps * hops]
-    chain_send, chain_recv, plane_send, plane_recv, term_send, term_recv, credit = rest[
+    chain_send, chain_recv, plane_send, plane_recv, term_send, term_recv, local, credit = rest[
         2 * steps * hops :
     ]
     cores = depth * width
@@ -82,7 +84,8 @@
         return carry
 
     lax.fori_loop(1, owners, greet, 0)
-    pl.semaphore_wait(barrier, owners - 1)
+    fetch = pltpu.make_async_copy(saved_in, saved, local.at[0])
+    fetch.start()
 
     def chain_block(step, way, hop):
         return chain[(step * 2 + way) * hops + hop - 1]
@@ -120,6 +123,10 @@
         )
 
     def serve(block, a_level):
+        fill_stage(block, a_level)
+        send_stage(a_level)
+
+    def fill_stage(block, a_level):
         source = owner_of(lane, a_level)
 
         def pick(offset, way):
@@ -136,6 +143,7 @@
 
         lax.fori_loop(1, lanes, fill, 0)
 
+    def send_stage(a_level):
         def send(offset, carry):
             plane_copy(offset, a_level).start()
             return carry
@@ -161,30 +169,36 @@
 
         lax.fori_loop(0, steps * subs, one, 0)
 
-    def project(step, half):
-        group = step * halves + half
-
-        def one(place, carry):
-            sub = half * batch + place
-            total = jnp.zeros((dim, 2 * dim), F32)
-            for j in range(count):
+    def turn(sub):
+        for j in range(count):
+            kept = saved[steps - 1, sub, j].reshape(2 * dim, dim)
+            saved_t[sub, :, 2 * dim * j : 2 * dim * (j + 1)] = kept.T
+
+    def project(step, sub):
+        total = jnp.zeros((dim, 2 * dim), F32)
+        for j in range(count):
+            lam_re = hist[step, sub + 1, j, 0]
+            lam_im = hist[step, sub + 1, j, 1]
+            both = jnp.concatenate(
+                [
+                    jnp.concatenate([lam_re, lam_im], axis=1),
+                    jnp.concatenate([lam_im, -lam_re], axis=1),
+                ],
+                axis=0,
+            )
+            if step == steps - 1:
+                kept_t = saved_t[sub, :, 2 * dim * j : 2 * dim * (j + 1)]
+                total = total + dot(kept_t, both)
+            else:
                 kept = saved[step, sub, j].reshape(2 * dim, dim)
-                lam_re = hist[step, sub + 1, j, 0]
-                lam_im = hist[step, sub + 1, j, 1]
-                both = jnp.concatenate(
-                    [
-                        jnp.concatenate([lam_re, lam_im], axis=1),
-                        jnp.concatenate([lam_im, -lam_re], axis=1),
-                    ],
-                    axis=0,
-                )
                 total = total + lax.dot_general(
                     kept, both, (((0,), (0,)), ((), ())), preferred_element_type=F32
                 )
-            terms[place] = total
-            return carry
-
-        lax.fori_loop(0, batch, one, 0)
+        terms[sub % batch] = total
+        if sub % batch == batch - 1:
+            spread(step * halves + sub // batch)
+
+    def spread(group):
         for target in range(owners):
             term_stage[group, target] = jnp.concatenate(
                 [terms[i, target * rows : (target + 1) * rows] for i in range(batch)], axis=0
@@ -210,7 +224,11 @@
         for offset in range(1, owners):
             total = total + term_inbox[group, offset - 1].astype(F32)
         for i in range(batch):
-            grad[group * batch + i] = total[i * rows : (i + 1) * rows]
+            for row in range(rows):
+                for part in range(2):
+                    grad[row, group * batch + i, part : part + 1, :] = total[
+                        i * rows + row : i * rows + row + 1, part * dim : (part + 1) * dim
+                    ]
         pltpu.make_async_copy(everything, everything, term_send.at[group]).wait()
 
     def couple(step, state):
@@ -273,6 +291,9 @@
 
         lax.fori_loop(half * batch, (half + 1) * batch, one, 0)
 
+    prepare()
+    fill_stage(adjoint, level)
+    pl.semaphore_wait(barrier, owners - 1)
     for step in range(steps):
         state = adjoint if step == 0 else hist.at[step - 1, subs]
         for way in range(2):
@@ -283,12 +304,22 @@
 
         if step > 0:
             pl.semaphore_wait(credit, lanes - 1)
-        serve(state, level)
+            fill_stage(state, level)
+        send_stage(level)
         if step == 0:
-            prepare()
-        else:
-            for half in range(halves):
-                project(step - 1, half)
+            fetch.wait()
+        beside = [[] for _ in range(depth)]
+        for sub in range(subs):
+            beside[sub * depth // subs].append(sub)
+
+        def aside(place):
+            for sub in beside[place]:
+                if step > 0:
+                    project(step - 1, sub)
+                if step == 0:
+                    turn(sub)
+
+        aside(0)
         for hop in range(1, depth):
             for way in range(2):
 
@@ -303,6 +334,8 @@
                             chain_copy(step, way, hop + 1, block).start()
 
                     serve(block, from_level(way, hop))
+
+            aside(hop)
 
         def collect(offset, carry):
             for a_level in range(depth):
@@ -331,7 +364,11 @@
         for half in range(halves):
             rotate(step, half)
             if step == steps - 1:
-                project(step, half)
+                for sub in range(half * batch, (half + 1) * batch):
+                    project(step, sub)
+                    if sub == subs - 1:
+                        result = pltpu.make_async_copy(hist.at[step, subs], out, local.at[1])
+                        result.start()
 
         def settle(offset, carry):
             for a_level in range(depth):
@@ -346,7 +383,7 @@
                 def _(way=way, hop=hop):
                     chain_copy(step, way, hop, chain_block(step, way, hop)).wait_send()
 
-    out[...] = hist[steps - 1, subs]
+    result.wait()
     for group in range(steps * halves):
         finish(group)
 
@@ -392,15 +429,16 @@
         out_specs=vmem,
     )(higher, lower)
     block = adjoint.shape
+    hbm = pl.BlockSpec(memory_space=pl.ANY)
     hops = depth - 1
     state, grad = pl.pallas_call(
         functools.partial(kernel, (nodes, depth, width, count, modes, steps, subs, dim, halves)),
         out_shape=(
             jax.ShapeDtypeStruct(block, BF16),
-            jax.ShapeDtypeStruct((steps * subs, rows, 2 * dim), F32),
+            jax.ShapeDtypeStruct((rows, steps * subs, 2, dim), F32),
         ),
-        in_specs=[smem] * 6 + [vmem] * 4,
-        out_specs=(vmem, vmem),
+        in_specs=[smem] * 6 + [vmem, hbm, vmem, vmem],
+        out_specs=(hbm, vmem),
         scratch_shapes=[
             pltpu.VMEM((steps * subs, 2 * dim, 2 * dim), BF16),
             pltpu.VMEM((steps * subs, 2 * dim, 2 * dim), BF16),
@@ -410,6 +448,8 @@
             pltpu.VMEM((batch, dim, 2 * dim), F32),
             pltpu.VMEM((steps * halves, owners, batch * rows, 2 * dim), BF16),
             pltpu.VMEM((steps * halves, owners - 1, batch * rows, 2 * dim), BF16),
+            pltpu.VMEM(saved.shape, BF16),
+            pltpu.VMEM((subs, dim, count * 2 * dim), BF16),
             *[pltpu.VMEM(block, BF16) for _ in range(2 * steps * hops)],
             pltpu.SemaphoreType.DMA((steps, 2, hops)),
             pltpu.SemaphoreType.DMA((steps, 2, hops)),
@@ -417,14 +457,14 @@
             pltpu.SemaphoreType.DMA((owners,)),
             pltpu.SemaphoreType.DMA((steps * halves,)),
             pltpu.SemaphoreType.DMA((steps * halves,)),
+            pltpu.SemaphoreType.DMA((2,)),
             pltpu.SemaphoreType.REGULAR,
         ],
         compiler_params=pltpu.CompilerParams(
             collective_id=0, has_side_effects=True, vmem_limit_bytes=63_000_000
         ),
     )(picks, higher, lower, ladder, rates, decay, adjoint, saved, propagators, coupling)
-    gradient = jnp.swapaxes(grad, 0, 1).reshape(rows, steps * subs, 2, dim)
-    return state, gradient
+    return state, grad
 
 
 def solution(mesh):

time: 138 us -> 136 us (0.986)
  Pallas kernels: 134 us -> 132 us
    pallas_call x1, Pallas kernels: 132 us -> 130 us  [body(): pl.pallas_call(functools.partial(kernel, (nodes, depth, width, count, mod...]
where the time goes in v4:
time: 136 us
  Pallas kernels  132 us (97%)
  local copies, waits for them, and re-layouts  3.26 us (2%)
    pallas_call x1, Pallas kernels, body(): pl.pallas_call(functools.partial(kernel, (nodes, depth, width, count, mod...  130 us
    unnamed x2, local copies, waits for them, and re-layouts  3.26 us

profile of v4, /device:TPU:0, one launch (start us, length us, event | category | flops | bytes accessed | tf_op | source)
XLA Modules:
  0.0 135.7 jit_solution(15502849930869305119)
XLA Ops:
  0.6 1.5 %shard_map.104.picks = s32[64,32]{1,0:T(8,128)} custom-call(s32[4,256]{1,0:T(4,128)} %bitcast.3, s32[4,256]{1,0:T(4,128)} %bitcast.5), custom_call_target="tpu_custom_call" | custom-call | tf_op jit(solution)/shard_map/pallas_call | solution.py:425
  2.1 130.3 %shard_map.105 = (bf16[8,2,128,128]{3,2,1,0:T(8,128)(2,1)}, f32[4,8,2,128]{3,2,1,0:T(2,128)}) custom-call(s32[64,32]{1,0:T(8,128)} %shard_map.104.picks, s32[4,256]{1,0:T(4,128)} %bitcast.4, s32[4,256]{1,0:T(4,128)} %bitcast.6, s32[2,4,8]{2,1,0:T(4,128)} %bitcast.7, f32[2,4]{1,0:T(2,128)} %rates.1, f32[8]{0:T(128)} %decay.1, ...), custom_call_target="tpu_custom_call" | custom-call | tf_op jit(solution)/shard_map/pallas_call | solution.py:434
  132.4 1.9 %copy.13 = bf16[8,2,128,128]{3,2,1,0:T(8,128)(2,1)} copy(bf16[8,2,128,128]{3,2,1,0:T(8,128)(2,1)} %get-tuple-element.4) | data formatting | bytes 1048576
  134.3 1.4 %copy.14 = f32[4,8,2,128]{3,2,1,0:T(2,128)} copy(f32[4,8,2,128]{3,2,1,0:T(2,128)} %get-tuple-element.5) | data formatting | bytes 65536

commit v5 on v4

--- a/solution.py
+++ b/solution.py
@@ -60,7 +60,10 @@
     lane = node * width + column
 
     def lane_of(offset):
-        return lax.rem(lane + offset, lanes)
+        pair = 2 if nodes % 2 == 0 else 1
+        far = lax.rem(node // pair + offset // (pair * width), nodes // pair)
+        near = lax.rem(node + offset // width, pair)
+        return (far * pair + near) * width + lax.rem(column + offset, width)
 
     def lane_id(other):
         return (other // width, level * width + other % width)

time: 136 us -> 136 us (level)
  no operation moved by 1% of the time
where the time goes in v5:
time: 136 us
  Pallas kernels  132 us (97%)
  local copies, waits for them, and re-layouts  3.26 us (2%)
    pallas_call x1, Pallas kernels, body(): pl.pallas_call(functools.partial(kernel, (nodes, depth, width, count, mod...  130 us
    unnamed x2, local copies, waits for them, and re-layouts  3.26 us

profile of v5, /device:TPU:0, one launch (start us, length us, event | category | flops | bytes accessed | tf_op | source)
XLA Modules:
  0.0 135.6 jit_solution(16151542872957868212)
XLA Ops:
  0.6 1.5 %shard_map.104.picks = s32[64,32]{1,0:T(8,128)} custom-call(s32[4,256]{1,0:T(4,128)} %bitcast.3, s32[4,256]{1,0:T(4,128)} %bitcast.5), custom_call_target="tpu_custom_call" | custom-call | tf_op jit(solution)/shard_map/pallas_call | solution.py:428
  2.1 130.2 %shard_map.105 = (bf16[8,2,128,128]{3,2,1,0:T(8,128)(2,1)}, f32[4,8,2,128]{3,2,1,0:T(2,128)}) custom-call(s32[64,32]{1,0:T(8,128)} %shard_map.104.picks, s32[4,256]{1,0:T(4,128)} %bitcast.4, s32[4,256]{1,0:T(4,128)} %bitcast.6, s32[2,4,8]{2,1,0:T(4,128)} %bitcast.7, f32[2,4]{1,0:T(2,128)} %rates.1, f32[8]{0:T(128)} %decay.1, ...), custom_call_target="tpu_custom_call" | custom-call | tf_op jit(solution)/shard_map/pallas_call | solution.py:437
  132.3 1.9 %copy.13 = bf16[8,2,128,128]{3,2,1,0:T(8,128)(2,1)} copy(bf16[8,2,128,128]{3,2,1,0:T(8,128)(2,1)} %get-tuple-element.4) | data formatting | bytes 1048576
  134.2 1.4 %copy.14 = f32[4,8,2,128]{3,2,1,0:T(2,128)} copy(f32[4,8,2,128]{3,2,1,0:T(2,128)} %get-tuple-element.5) | data formatting | bytes 65536
